TPU v7x, 32 devices: a whole 2x2x4 slice. The times are simulated.
32 devices in a mesh: row: 4 (over z), col: 8 (over y, x, core).
Axes of the slice: x: 2, y: 2, z: 4, core: 2. Of those that a mesh axis runs over, the one named last changes fastest.
Arguments:
- customer_inputs: bfloat16 [32768, 1024], P(('row', 'col')), may hold values from -6 to 6
- candidate_inputs: bfloat16 [32768, 1024], P(('row', 'col')), may hold values from -6 to 6
- affinity_sharpness: bfloat16 [32768], P(('row', 'col')), may hold values from 4 to 40
- correct_candidate_index: int32 [32768], P(('row', 'col')), may hold values from 0 to 4095
- customer_initial_weights: bfloat16 [1024, 512], replicated, may hold values from -0.1875 to 0.1875
- customer_final_weights: bfloat16 [512, 256], replicated, may hold values from -0.25 to 0.25
- candidate_initial_weights: bfloat16 [1024, 512], replicated, may hold values from -0.1875 to 0.1875
- candidate_final_weights: bfloat16 [512, 256], replicated, may hold values from -0.25 to 0.25
Outputs:
- loss: float32 [], replicated
- grad_user_first: float32 [1024, 512], replicated
- grad_user_second: float32 [512, 256], replicated
- grad_item_first: float32 [1024, 512], replicated
- grad_item_second: float32 [512, 256], replicated
Inputs may be any that keep to these rules, and one draw needn't show every extreme that they name: correct_candidate_index[u] indexes the items of u's group in the order of the steps.
All inputs are finite; a program needn't handle non-finite values.
Results may differ from a plain program's by a relative error of at most 0.015.
Values may be sent and summed in bfloat16 or wider, within the bound.
A program may use at most 128 MiB of HBM per device.

v0:
```python
import jax
import jax.numpy as jnp
from jax import lax
from jax.sharding import PartitionSpec as P

EPS = 1e-06


def tower_forward(feats, first, second):
    pre = jnp.dot(feats, first, preferred_element_type=jnp.float32)
    hidden = jax.nn.relu(pre).astype(jnp.bfloat16)
    out = jnp.dot(hidden, second, preferred_element_type=jnp.float32)
    inv = lax.rsqrt(jnp.mean(out * out, axis=-1, keepdims=True) + EPS)
    return ((out * inv).astype(jnp.bfloat16), (pre, hidden, out, inv))


def tower_backward(feats, second, saved, grad_vec):
    pre, hidden, out, inv = saved
    grad = grad_vec.astype(jnp.float32)
    normed = out * inv
    grad_out = (inv * (grad - normed * jnp.mean(grad * normed, axis=-1, keepdims=True))).astype(
        jnp.bfloat16
    )
    grad_second = jnp.dot(hidden.T, grad_out, preferred_element_type=jnp.float32)
    grad_hidden = jnp.dot(grad_out, second.T, preferred_element_type=jnp.float32)
    grad_pre = jnp.where(pre > 0, grad_hidden, 0.0).astype(jnp.bfloat16)
    grad_first = jnp.dot(feats.T, grad_pre, preferred_element_type=jnp.float32)
    return (grad_first, grad_second)


def positive_pair_logit(
    shopper_vector, gathered_entries, affinity_sharpness, correct_candidate_index, resident_table
):
    latent_code = shopper_vector.shape[-1]
    coolness_fp32_number = affinity_sharpness.astype(jnp.float32)
    affinity_matrix = (
        coolness_fp32_number[:, None]
        * jnp.einsum(
            "ue,ie->ui", shopper_vector, gathered_entries, preferred_element_type=jnp.float32
        )
        / latent_code
    )
    lse = jax.nn.logsumexp(affinity_matrix, axis=1)
    columns = lax.broadcasted_iota(jnp.int32, affinity_matrix.shape, 1)
    target_column = columns == correct_candidate_index[:, None]
    picked = jnp.sum(jnp.where(target_column, affinity_matrix, 0.0), axis=1)
    softmax_likelihood = jnp.exp(affinity_matrix - lse[:, None])
    sensitivity_of_affinities = (
        (softmax_likelihood - target_column.astype(jnp.float32))
        * (coolness_fp32_number / (latent_code * resident_table))[:, None]
    ).astype(jnp.bfloat16)
    customer_derivative = jnp.dot(
        sensitivity_of_affinities, gathered_entries, preferred_element_type=jnp.float32
    )
    return (lse, sensitivity_of_affinities, customer_derivative, jnp.sum(lse - picked))


def body(
    customer_inputs,
    candidate_inputs,
    affinity_sharpness,
    correct_candidate_index,
    customer_initial_weights,
    customer_final_weights,
    candidate_initial_weights,
    candidate_final_weights,
):
    resident_table = customer_inputs.shape[0]
    shopper_vector, user_saved = tower_forward(
        customer_inputs, customer_initial_weights, customer_final_weights
    )
    offered_thing_vector, item_saved = tower_forward(
        candidate_inputs, candidate_initial_weights, candidate_final_weights
    )
    latent_code = shopper_vector.shape[-1]
    gathered_entries = lax.all_gather(offered_thing_vector, "row", axis=0, tiled=True)
    lse, sensitivity_of_affinities, customer_derivative, loss_local = positive_pair_logit(
        shopper_vector,
        gathered_entries,
        affinity_sharpness,
        correct_candidate_index,
        resident_table,
    )
    all_users, all_scales = (
        lax.all_gather(shopper_vector, "row", axis=0, tiled=True),
        lax.all_gather(affinity_sharpness, "row", axis=0, tiled=True),
    )
    all_positive = lax.all_gather(correct_candidate_index, "row", axis=0, tiled=True)
    all_lse = lax.all_gather(lse, "row", axis=0, tiled=True)
    coolness_fp32_number = all_scales.astype(jnp.float32)
    affinity_matrix = (
        coolness_fp32_number[:, None]
        * jnp.einsum(
            "ue,ie->ui", all_users, offered_thing_vector, preferred_element_type=jnp.float32
        )
        / latent_code
    )
    start = lax.axis_index("row") * resident_table
    columns = lax.broadcasted_iota(jnp.int32, affinity_matrix.shape, 1) + start
    target_column = columns == all_positive[:, None]
    softmax_likelihood = jnp.exp(affinity_matrix - all_lse[:, None])
    group_dlogits = (
        (softmax_likelihood - target_column.astype(jnp.float32))
        * (coolness_fp32_number / (latent_code * resident_table))[:, None]
    ).astype(jnp.bfloat16)
    candidate_derivative = jnp.einsum(
        "ui,ue->ie", group_dlogits, all_users, preferred_element_type=jnp.float32
    )
    grad_user_first, grad_user_second = tower_backward(
        customer_inputs,
        customer_final_weights,
        user_saved,
        customer_derivative.astype(jnp.bfloat16),
    )
    grad_item_first, grad_item_second = tower_backward(
        candidate_inputs,
        candidate_final_weights,
        item_saved,
        candidate_derivative.astype(jnp.bfloat16),
    )
    summed = lax.psum(
        (grad_user_first, grad_user_second, grad_item_first, grad_item_second, loss_local),
        ("row", "col"),
    )
    users_total = resident_table * lax.axis_size("row") * lax.axis_size("col")
    return (summed[4] / users_total, summed[0], summed[1], summed[2], summed[3])


def solution(mesh):
    placed = (
        P(("row", "col"), None),
        P(("row", "col"), None),
        P(("row", "col")),
        P(("row", "col")),
        P(),
        P(),
        P(),
        P(),
    )
    return jax.shard_map(
        body, mesh=mesh, in_specs=placed, out_specs=(P(), P(), P(), P(), P()), check_vma=False
    )
```

profile of v0, /device:TPU:0, one launch (start us, length us, event | category | flops | bytes accessed | tf_op | source)
XLA Modules:
  0.0 292.9 jit_solution(12754401451739418101)
XLA Ops:
  7.2 3.3 %fusion.26 = f32[1024,512]{1,0:T(8,128)S(1)} fusion(bf16[1024,1024]{1,0:T(8,128)(2,1)} %param.9, bf16[1024,512]{1,0:T(8,128)(2,1)} %param.14), kind=kOutput, calls=%fused_computation.56 | convolution fusion | flops 1073741824 | bytes 5242880 | tf_op jit(solution)/shard_map/dot_general | solution.py:10
  10.5 1.3 copy-done.3
  11.8 0.5 multiply_reduce_fusion
  12.4 0.9 multiply_convert_fusion.5
  13.4 2.5 fusion.25
  15.9 1.3 copy-done.4
  17.2 0.5 multiply_reduce_fusion.1
  17.7 0.9 copy-done.1
  18.7 0.9 multiply_convert_fusion.6
  19.7 14.1 %all_gather.16 = bf16[4096]{0:T(1024)(128)(2,1)S(1)} all-gather(bf16[1024]{0:T(1024)(128)(2,1)S(1)} %copy-done.14), channel_id=1, replica_groups=mesh['row'=4,'col'=8] {'row'}, dimensions={0}, use_global_device_ids=true | all-gather | bytes 10240 | tf_op jit(solution)/shard_map/all_gather | solution.py:86
  33.8 13.6 %all_gather.19 = s32[4096]{0:T(1024)S(1)} all-gather(s32[1024]{0:T(1024)S(1)} %copy-done.15), channel_id=1, replica_groups=mesh['row'=4,'col'=8] {'row'}, dimensions={0}, use_global_device_ids=true | all-gather | bytes 20480 | tf_op jit(solution)/shard_map/all_gather | solution.py:88
  47.4 14.8 %all-gather.3.cloned.1.call-done = bf16[4096,256]{0,1:T(8,128)(2,1)} async-done(((bf16[1024,256]{0,1:T(8,128)(2,1)}), bf16[4096,256]{0,1:T(8,128)(2,1)}) %all-gather.3.cloned.1.call-update) | async-done | bytes 2097168 | tf_op jit(solution)/shard_map/all_gather | solution.py:76
  62.2 4.3 %fusion = (f32[1024]{0:T(1024)S(1)}, f32[1024,4096]{1,0:T(8,128)S(1)}) fusion(f32[1024]{0:T(1024)S(1)} %convert_element_type.54, bf16[1024,256]{0,1:T(8,128)(2,1)} %multiply_convert_fusion.6, bf16[4096,256]{0,1:T(8,128)(2,1)} %all-gather.3.cloned.1.call-done), kind=kOutput, calls=%fused_computation.6 | convolution fusion | flops 2160065536 | bytes 19406848 | tf_op jit(solution)/shard_map/ue,ie->ui/dot_general | solution.py:38
  66.5 6.9 %select_reduce_fusion = (f32[1024]{0:T(1024)S(1)}, f32[1024]{0:T(1024)S(1)}) fusion(f32[1024,4096]{1,0:T(8,128)S(1)} %get-tuple-element.28, s32[1024]{0:T(1024)S(1)} %copy-done.15, f32[1024]{0:T(1024)S(1)} %convert_element_type.54, f32[1024]{0:T(1024)S(1)} %is-finite_select_fusion), kind=kLoop, calls=%fused_computation.2 | loop fusion | flops 29358080 | bytes 16797696 | tf_op jit(solution)/shard_map/reduce_sum | solution.py:46
  73.3 0.6 subtract_reduce_fusion
  74.0 13.8 %all_gather.18 = f32[4096]{0:T(1024)S(1)} all-gather(f32[1024]{0:T(1024)S(1)} %get-tuple-element.22), channel_id=1, replica_groups=mesh['row'=4,'col'=8] {'row'}, dimensions={0}, use_global_device_ids=true | all-gather | bytes 20480 | tf_op jit(solution)/shard_map/all_gather | solution.py:89
  87.8 7.9 %fusion.5 = (f32[1024]{0:T(1024)S(1)}, bf16[1024,256]{0,1:T(8,128)(2,1)S(1)}) fusion(f32[1024,256]{0,1:T(8,128)S(1)} %copy-done.2, f32[1024]{0:T(1024)S(1)} %add_rsqrt_fusion.1, bf16[4096,256]{0,1:T(8,128)(2,1)S(1)} %copy-done.6, f32[1024,4096]{1,0:T(8,128)S(1)} %get-tuple-element.28, f32[1024]{0:T(1024)S(1)} %broadcast_multiply_fusion.1, ...), kind=kOutput, calls=%fused_computation.21 | convolution fusion | flops 2182347776 | bytes 20471808 | tf_op jit(solution)/shard_map/dot_general | solution.py:52
  96.0 0.8 copy-done.7
  96.7 0.8 copy-done.5
  97.5 1.3 fusion.13
  98.8 4.7 %convolution_bitcast_fusion.1 = f32[1024,512]{0,1:T(8,128)} fusion(bf16[1024,1024]{1,0:T(8,128)(2,1)S(1)} %copy-done, f32[1024,512]{1,0:T(8,128)} %copy-done.4, bf16[1024,256]{0,1:T(8,128)(2,1)} %copy-done.7, bf16[512,256]{1,0:T(8,128)(2,1)S(1)} %copy-done.11), kind=kOutput, calls=%fused_computation.14 | convolution fusion | flops 1343750144 | bytes 7077888 | tf_op jit(solution)/shard_map/dot_general | solution.py:27
  103.5 5.5 %all-gather.5.cloned.1.call-done = bf16[4096,256]{0,1:T(8,128)(2,1)} async-done(((bf16[1024,256]{0,1:T(8,128)(2,1)}), bf16[4096,256]{0,1:T(8,128)(2,1)}) %all-gather.5.cloned.1.call-update) | async-done | bytes 2097168 | tf_op jit(solution)/shard_map/all_gather | solution.py:85
  109.1 10.3 %fusion.8 = (f32[1024]{0:T(1024)S(1)}, bf16[1024,256]{0,1:T(8,128)(2,1)}) fusion(f32[1024,256]{0,1:T(8,128)S(1)} %get-tuple-element.26, f32[1024]{0:T(1024)S(1)} %add_rsqrt_fusion, bf16[4096,256]{0,1:T(8,128)(2,1)} %all-gather.5.cloned.1.call-done, f32[4096]{0:T(1024)S(1)} %broadcast_multiply_fusion, s32[1024]{0:T(1024)S(1)} %iota_add_fusion, ...), kind=kOutput, calls=%fused_computation.24 | convolution fusion | flops 4330355712 | bytes 3747840 | tf_op jit(solution)/shard_map/ui,ue->ie/dot_general | solution.py:106
  119.4 2.1 fusion.10
  121.4 5.4 %convolution_bitcast_fusion = f32[1024,512]{0,1:T(8,128)} fusion(bf16[1024,1024]{1,0:T(8,128)(2,1)} %param.9, f32[1024,512]{1,0:T(8,128)} %copy-done.3, bf16[1024,256]{0,1:T(8,128)(2,1)} %fusion.10, bf16[512,256]{1,0:T(8,128)(2,1)S(1)} %copy-done.13), kind=kOutput, calls=%fused_computation.13 | convolution fusion | flops 1343750144 | bytes 7077888 | tf_op jit(solution)/shard_map/dot_general | solution.py:27
  126.8 2.9 fusion.15
  129.7 39.7 %psum.35 = f32[]{:T(128)} all-reduce(f32[]{:T(128)} %get-tuple-element.21), channel_id=1, replica_groups=mesh['row'=4,'col'=8] {'row','col'}, use_global_device_ids=true, to_apply=%region_6.7 | all-reduce | flops 1 | bytes 8 | tf_op jit(solution)/shard_map/psum | solution.py:121
  170.0 107.8 %all-reduce.3.cloned.1.call-done = (f32[1024,512]{0,1:T(8,128)}, f32[512,256]{1,0:T(8,128)}, f32[1024,512]{0,1:T(8,128)}, f32[512,256]{1,0:T(8,128)}) async-done(((f32[1024,512]{0,1:T(8,128)}, f32[512,256]{1,0:T(8,128)}, f32[1024,512]{0,1:T(8,128)}, f32[512,256]{1,0:T(8,128)}), (f32[1024,512]{0,1:T(8,128)}, f32[512,256]{1,0:T(8,128)}, f32[1024,512]{0,1:T(8,128)}, ...) | async-done | bytes 5242896 | tf_op jit(solution)/shard_map/psum | solution.py:121
  277.8 2.9 copy.15
  280.7 3.0 %copy.16 = f32[1024,512]{1,0:T(8,128)} copy(f32[1024,512]{0,1:T(8,128)} %get-tuple-element.19) | data formatting | bytes 4194304
  283.6 0.8 copy.21
  284.4 0.8 copy.22
  (44 shorter events, 0.5 us)
Async XLA Ops:
  7.2 6.2 %copy-start = (bf16[1024,1024]{1,0:T(8,128)(2,1)S(1)}, bf16[1024,1024]{1,0:T(8,128)(2,1)}, u32[]{:S(2)}) copy-start(bf16[1024,1024]{1,0:T(8,128)(2,1)} %param.8) | copy-start | bytes 6291460
  7.2 4.7 %copy-start.12 = (bf16[512,256]{1,0:T(8,128)(2,1)S(1)}, bf16[512,256]{1,0:T(8,128)(2,1)}, u32[]{:S(2)}) copy-start(bf16[512,256]{1,0:T(8,128)(2,1)} %param.15) | copy-start | bytes 786436
  7.2 55.0 %all-gather.3.cloned.1.call-start = ((), (), s32[]{:S(2)}) async-start(), calls=%async_computation | async-start | bytes 2621440 | tf_op jit(solution)/shard_map/all_gather | solution.py:76
  10.5 1.3 copy-start.3
  13.3 3.9 %copy-start.11 = (bf16[512,256]{1,0:T(8,128)(2,1)S(1)}, bf16[512,256]{1,0:T(8,128)(2,1)}, u32[]{:S(2)}) copy-start(bf16[512,256]{1,0:T(8,128)(2,1)} %param.13) | copy-start | bytes 786436
  13.3 95.8 %all-gather.5.cloned.1.call-start = ((), (), s32[]{:S(2)}) async-start(), calls=%async_computation.1 | async-start | bytes 2621440 | tf_op jit(solution)/shard_map/all_gather | solution.py:85
  15.9 1.3 copy-start.4
  17.2 2.4 copy-start.14
  17.2 16.6 %copy-start.15 = (s32[1024]{0:T(1024)S(1)}, s32[1024]{0:T(1024)}, u32[]{:S(2)}) copy-start(s32[1024]{0:T(1024)} %param.11) | copy-start | bytes 12292
  17.7 1.0 copy-start.1
  19.6 258.2 %all-reduce.3.cloned.1.call-start = ((), (), s32[]{:S(2)}) async-start(), calls=%async_computation.2 | async-start | bytes 10485760 | tf_op jit(solution)/shard_map/psum | solution.py:121
  66.4 21.3 %copy-start.2 = (f32[1024,256]{0,1:T(8,128)S(1)}, f32[1024,256]{0,1:T(8,128)}, u32[]{:S(2)}) copy-start(f32[1024,256]{0,1:T(8,128)} %copy-done.1) | copy-start | bytes 3145732
  66.4 21.3 %copy-start.6 = (bf16[4096,256]{0,1:T(8,128)(2,1)S(1)}, bf16[4096,256]{0,1:T(8,128)(2,1)}, u32[]{:S(2)}) copy-start(bf16[4096,256]{0,1:T(8,128)(2,1)} %all-gather.3.cloned.1.call-done) | copy-start | bytes 6291460
  95.7 1.8 copy-start.5
  95.9 0.8 copy-start.7
  119.3 2.1 copy-start.13
  121.4 5.4 %copy-start.8 = (bf16[1024,256]{0,1:T(8,128)(2,1)S(1)}, bf16[1024,256]{0,1:T(8,128)(2,1)}, u32[]{:S(2)}) copy-start(bf16[1024,256]{0,1:T(8,128)(2,1)} %fusion.10) | copy-start | bytes 1572868
  280.7 3.0 %copy-start.10 = (f32[512,256]{1,0:T(8,128)S(1)}, f32[512,256]{1,0:T(8,128)}, u32[]{:S(2)}) copy-start(f32[512,256]{1,0:T(8,128)} %get-tuple-element.35) | copy-start | bytes 1572868
  280.7 3.8 %copy-start.9 = (f32[512,256]{1,0:T(8,128)S(1)}, f32[512,256]{1,0:T(8,128)}, u32[]{:S(2)}) copy-start(f32[512,256]{1,0:T(8,128)} %get-tuple-element.37) | copy-start | bytes 1572868
Sparse Core Ops, SparseCore 0:
  13.4 48.7 all-gather.2
  64.3 44.7 all-gather.4
  129.8 147.9 all-reduce.2
where the time goes:
time: 293 us
  waiting for transfers between devices  128 us (44%)
  blocking collectives  81.1 us (28%)
  matrix products  43.5 us (15%)
  between operations  15.7 us (5%)
  local copies, waits for them, and re-layouts  12.6 us (4%)
  other arithmetic  11.6 us (4%)
    psum x1, waiting for transfers between devices, body(): lax.psum((grad_user_first, grad_user_second, grad_item_first, grad_item_s...  108 us
    psum x1, blocking collectives, body(): lax.psum((grad_user_first, grad_user_second, grad_item_first, grad_item_s...  39.7 us
    all_gather x1, waiting for transfers between devices, body(): lax.all_gather(offered_thing_vector, 'row', axis=0, tiled=True)  14.8 us
    all_gather x1, blocking collectives, body(): lax.all_gather(affinity_sharpness, 'row', axis=0, tiled=True)  14.1 us
    all_gather x1, blocking collectives, body(): all_lse = lax.all_gather(lse, 'row', axis=0, tiled=True)  13.8 us
    all_gather x1, blocking collectives, body(): lax.all_gather(correct_candidate_index, 'row', axis=0, tiled=True)  13.6 us
    unnamed x36, local copies, waits for them, and re-layouts  12.6 us
    dot_general x1, matrix products, body(): jnp.einsum('ui,ue->ie', group_dlogits, all_users, preferred_element_type=...  10.3 us
  transfers between devices with their start and end apart: 3, of which 3 were waited for; matrix products, arithmetic and copies ran while one was open for 10% of the time, Pallas kernels for 0%

commit v1 on v0

v1 whole, which is shorter than its diff:
```python
import functools

import jax
import jax.numpy as jnp
from jax import lax
from jax.experimental import pallas as pl
from jax.experimental.pallas import tpu as pltpu
from jax.sharding import PartitionSpec as P

EPS = 1e-06
MESH = pl.DeviceIdType.MESH
F32 = jnp.float32
BF16 = jnp.bfloat16
TILE = 256


def mm(a, b, ca=1, cb=0):
    return lax.dot_general(a, b, (((ca,), (cb,)), ((), ())), preferred_element_type=F32)


def kernel(
    R, C, T, M, F, H, E, hold,
    xu_hbm, xi_hbm, sharp_ref, pos_ref, w1u_hbm, w2u_hbm, w1i_hbm, w2i_hbm,
    fin_hbm, loss_ref,
    X, W1, W2, HID, OUT, U, IT, EX, D, GI, RR, RL, GU, GV, GP, LS, PK,
    B, P1, P2, S2, P3, FIN, L0, L1, L2, L3,
    in_sem, out_sem, ag_send, ag_recv, rs_send, rs_recv,
    c1s, c1r, c2s, c2r, c3s, c3r, c4s, c4r, c5s, c5r, c6s, c6r, ls, lr,
):
    C2 = C // 2
    r = lax.axis_index("row")
    c = lax.axis_index("col")
    core = lax.rem(c, 2)
    chip = c // 2
    partner = chip * 2 + (1 - core)
    NH = C2 * R * T
    NT = 2 * NH
    RT = R * T
    loads = []
    for t, (xh, w1h, w2h) in enumerate(((xi_hbm, w1i_hbm, w2i_hbm), (xu_hbm, w1u_hbm, w2u_hbm))):
        for k, (src, dst) in enumerate(((w1h, W1.at[t]), (w2h, W2.at[t]), (xh, X.at[t]))):
            loads.append(pltpu.make_async_copy(src, dst, in_sem.at[t, k]))
    for cp in loads:
        cp.start()

    barrier = pltpu.get_barrier_semaphore()
    for j in range(1, R):
        pl.semaphore_signal(barrier, inc=1, device_id=(lax.rem(r + j, R), c), device_id_type=MESH)
    for j in range(1, C2):
        pl.semaphore_signal(
            barrier, inc=1, device_id=(r, lax.rem(chip + j, C2) * 2 + core), device_id_type=MESH
        )
    pl.semaphore_signal(barrier, inc=1, device_id=(r, partner), device_id_type=MESH)

    def rows(i):
        return pl.ds(pl.multiple_of(i * TILE, TILE), TILE)

    def forward(t, put):
        def step(i, _):
            s = rows(i)
            pre = mm(X[t, s, :], W1[t])
            h = jnp.maximum(pre, 0.0).astype(BF16)
            HID[t, s, :] = h
            out = mm(h, W2[t])
            OUT[t, s, :] = out
            inv = lax.rsqrt(jnp.mean(out * out, axis=-1, keepdims=True) + EPS)
            put(s, (out * inv).astype(BF16))
            return 0

        lax.fori_loop(0, M // TILE, step, 0)

    for cp in loads[:3]:
        cp.wait()

    def put_item(s, v):
        IT[r, s, :] = v

    forward(0, put_item)
    pl.semaphore_wait(barrier, R + C2 - 1)

    def ag(b, right):
        d = 1 if right else 0
        return pltpu.make_async_remote_copy(
            src_ref=IT.at[b], dst_ref=IT.at[b], send_sem=ag_send.at[d, b], recv_sem=ag_recv.at[b],
            device_id=(r + 1 if right else r - 1, c), device_id_type=MESH,
        )

    @pl.when(r < R - 1)
    def _():
        ag(r, True).start()

    @pl.when(r > 0)
    def _():
        ag(r, False).start()

    for cp in loads[3:]:
        cp.wait()

    def put_user(s, v):
        U[s, :] = v

    forward(1, put_user)
    LS[...] = jnp.zeros_like(LS)
    PK[...] = jnp.zeros_like(PK)
    factor = sharp_ref[...].astype(F32) * (1.0 / E)
    positive = pos_ref[...]

    def score(b):
        def step(i, _):
            s = rows(i)
            logit = mm(IT[b, s, :], U[...], 1, 1) * factor
            item = lax.broadcasted_iota(jnp.int32, logit.shape, 0) + (b * M + i * TILE)
            e = jnp.exp(logit)
            if hold:
                EX[b, s, :] = e
            LS[...] += jnp.sum(e, axis=0, keepdims=True)
            PK[...] += jnp.sum(jnp.where(item == positive, logit, 0.0), axis=0, keepdims=True)
            return 0

        lax.fori_loop(0, M // TILE, step, 0)

    score(r)

    def arrive(d, _):
        lo = r - d
        hi = r + d

        @pl.when(lo >= 0)
        def _():
            ag(lo, True).wait_recv()

            @pl.when(r < R - 1)
            def _():
                ag(lo, True).start()

        @pl.when(hi < R)
        def _():
            ag(hi, False).wait_recv()

            @pl.when(r > 0)
            def _():
                ag(hi, False).start()

        def one(k, _):
            b = lo + k * (hi - lo)

            @pl.when(jnp.logical_and(b >= 0, b < R))
            def _():
                score(b)

            return 0

        lax.fori_loop(0, 2, one, 0)
        return 0

    lax.fori_loop(1, R, arrive, 0)

    L0[...] = jnp.full(L0.shape, jnp.sum(jnp.log(LS[...]) - PK[...]), F32)
    GU[...] = jnp.zeros_like(GU)
    rate = factor * (1.0 / M)
    norm = 1.0 / LS[...]

    def back(b):
        def step(i, _):
            s = rows(i)
            item = lax.broadcasted_iota(jnp.int32, (TILE, M), 0) + (b * M + i * TILE)
            hit = jnp.where(item == positive, 1.0, 0.0)
            e = EX[b, s, :] if hold else jnp.exp(mm(IT[b, s, :], U[...], 1, 1) * factor)
            d = ((e * norm - hit) * rate).astype(BF16)
            D[b, s, :] = d
            GI[b, s, :] = mm(d, U[...]).astype(BF16)
            return 0

        lax.fori_loop(0, M // TILE, step, 0)

    def rs(b, right):
        d = 1 if right else 0
        land = RR if right else RL
        return pltpu.make_async_remote_copy(
            src_ref=GI.at[b], dst_ref=land.at[b], send_sem=rs_send.at[b], recv_sem=rs_recv.at[d, b],
            device_id=(r + 1 if right else r - 1, c), device_id_type=MESH,
        )

    def leave(k, _):
        d = R - 1 - k
        lo = r - d
        hi = r + d

        def one(q, _):
            b = hi + q * (lo - hi)

            @pl.when(jnp.logical_and(b >= 0, b < R))
            def _():
                back(b)

            return 0

        lax.fori_loop(0, 2, one, 0)

        @pl.when(jnp.logical_and(hi < R, r == 0))
        def _():
            rs(hi, True).start()

        @pl.when(jnp.logical_and(lo >= 0, r == R - 1))
        def _():
            rs(lo, False).start()

        return 0

    lax.fori_loop(0, R - 1, leave, 0)

    def add_rows(dst, b, land):
        def step(i, _):
            s = rows(i)
            dst[b, s, :] = (dst[b, s, :].astype(F32) + land[b, s, :].astype(F32)).astype(BF16)
            return 0

        lax.fori_loop(0, M // TILE, step, 0)

    def relay(k):
        hi = R - 1 - k
        lo = k

        @pl.when(jnp.logical_and(hi > r, r > 0))
        def _():
            rs(hi, True).wait_recv()
            add_rows(GI, hi, RR)
            rs(hi, True).start()

        @pl.when(jnp.logical_and(lo < r, r < R - 1))
        def _():
            rs(lo, False).wait_recv()
            add_rows(GI, lo, RL)
            rs(lo, False).start()

    back(r)

    def user_grad(b, _):
        def step(i, _):
            s = rows(i)
            GU[s, :] += mm(D[b, :, s], IT[b], 0, 0)
            return 0

        lax.fori_loop(0, M // TILE, step, 0)
        return 0

    def backward_in(t, grad):
        def step(i, _):
            s = rows(i)
            g = grad(s)
            out = OUT[t, s, :]
            inv = lax.rsqrt(jnp.mean(out * out, axis=-1, keepdims=True) + EPS)
            n = out * inv
            go = (inv * (g - n * jnp.mean(g * n, axis=-1, keepdims=True))).astype(BF16)
            GV[s, :] = go
            gh = mm(go, W2[t], 1, 1)
            GP[s, :] = jnp.where(HID[t, s, :].astype(F32) > 0, gh, 0.0).astype(BF16)
            return 0

        lax.fori_loop(0, M // TILE, step, 0)

    def lay(t, base, height, i, v):
        for k in range(v.shape[1] // 128):
            part = v[:, k * 128 : (k + 1) * 128].astype(BF16).reshape(TILE // 16, 16, 128)
            B[t, pl.ds(base + k * (height // 16) + i * (TILE // 16), TILE // 16)] = part

    def backward_out(t):
        def second(i, _):
            lay(t, (F // 16) * (H // 128), H, i, mm(HID[t, :, rows(i)], GV[...], 0, 0))
            return 0

        lax.fori_loop(0, H // TILE, second, 0)

        def first(i, _):
            lay(t, 0, F, i, mm(X[t, :, rows(i)], GP[...], 0, 0))
            return 0

        lax.fori_loop(0, F // TILE, first, 0)

    def remote(src, dst, ss, rr, dev):
        return pltpu.make_async_remote_copy(
            src_ref=src, dst_ref=dst, send_sem=ss, recv_sem=rr, device_id=dev, device_id_type=MESH
        )

    half = core * NH
    mine = half + chip * RT
    tile0 = mine + r * T

    def cp1(t):
        return [remote(B.at[t, pl.ds((1 - core) * NH, NH)], P1.at[t], c1s.at[t], c1r.at[t], (r, partner))]

    def cp2(t):
        out = []
        for j in range(1, C2):
            to = lax.rem(chip + j, C2)
            out.append(remote(B.at[t, pl.ds(half + to * RT, RT)], P2.at[t, j - 1], c2s.at[t, j - 1],
                              c2r.at[t, j - 1], (r, to * 2 + core)))
        return out

    def cp3(t):
        out = []
        for j in range(1, R):
            to = lax.rem(r + j, R)
            out.append(remote(S2.at[t, pl.ds(to * T, T)], P3.at[t, j - 1], c3s.at[t, j - 1],
                              c3r.at[t, j - 1], (to, c)))
        return out

    def cp4(t):
        ref = FIN.at[t, pl.ds(tile0, T)]
        return [remote(ref, ref, c4s.at[t, j - 1], c4r.at[t, j - 1], (lax.rem(r + j, R), c))
                for j in range(1, R)]

    def cp4_in(t):
        out = []
        for j in range(1, R):
            ref = FIN.at[t, pl.ds(mine + lax.rem(r + R - j, R) * T, T)]
            out.append(remote(ref, ref, c4s.at[t, j - 1], c4r.at[t, j - 1], (lax.rem(r + j, R), c)))
        return out

    def cp5(t):
        ref = FIN.at[t, pl.ds(mine, RT)]
        return [remote(ref, ref, c5s.at[t, j - 1], c5r.at[t, j - 1],
                       (r, lax.rem(chip + j, C2) * 2 + core)) for j in range(1, C2)]

    def cp5_in(t):
        out = []
        for j in range(1, C2):
            ref = FIN.at[t, pl.ds(half + lax.rem(chip + C2 - j, C2) * RT, RT)]
            out.append(remote(ref, ref, c5s.at[t, j - 1], c5r.at[t, j - 1],
                              (r, lax.rem(chip + j, C2) * 2 + core)))
        return out

    def cp6(t):
        ref = FIN.at[t, pl.ds(half, NH)]
        return [remote(ref, ref, c6s.at[t], c6r.at[t], (r, partner))]

    def cp6_in(t):
        ref = FIN.at[t, pl.ds((1 - core) * NH, NH)]
        return [remote(ref, ref, c6s.at[t], c6r.at[t], (r, partner))]

    def start(cps):
        for cp in cps:
            cp.start()

    def arrived(cps):
        for cp in cps:
            cp.wait_recv()

    def sum1(t):
        arrived(cp1(t))

        def step(i, _):
            at = pl.ds(half + i * RT, RT)
            B[t, at] = (B[t, at].astype(F32) + P1[t, pl.ds(i * RT, RT)].astype(F32)).astype(BF16)
            return 0

        lax.fori_loop(0, C2, step, 0)
        start(cp2(t))

    def sum2(t):
        arrived(cp2(t))
        total = B[t, pl.ds(mine, RT)].astype(F32)
        for j in range(C2 - 1):
            total += P2[t, j].astype(F32)
        S2[t] = total.astype(BF16)
        start(cp3(t))

    def sum3(t):
        arrived(cp3(t))
        total = S2[t, pl.ds(r * T, T)].astype(F32)
        for j in range(R - 1):
            total += P3[t, j].astype(F32)
        FIN[t, pl.ds(tile0, T)] = total.astype(BF16)
        start(cp4(t))

    def share5(t):
        arrived(cp4_in(t))
        start(cp5(t))

    def share6(t):
        arrived(cp5_in(t))
        start(cp6(t))

    def finish(t):
        arrived(cp6_in(t))
        return pltpu.make_async_copy(FIN.at[t], fin_hbm.at[t], out_sem.at[t])

    loss1 = [remote(L0, L1, ls.at[0], lr.at[0], (r, partner))]
    loss2 = [remote(L2.at[0], L2.at[j], ls.at[j], lr.at[j], (r, lax.rem(chip + j, C2) * 2 + core))
             for j in range(1, C2)]
    loss3 = [remote(L3.at[0], L3.at[j], ls.at[C2 - 1 + j], lr.at[C2 - 1 + j], (lax.rem(r + j, R), c))
             for j in range(1, R)]

    start(loss1)
    relay(0)
    lax.fori_loop(0, R, user_grad, 0)
    if R > 2:
        relay(1)
    backward_in(1, lambda s: GU[s, :].astype(BF16).astype(F32))
    if R > 3:
        relay(2)
    backward_out(1)
    start(cp1(1))
    for k in range(3, R - 1):
        relay(k)
    arrived(loss1)
    L2[0] = L0[...] + L1[...]
    start(loss2)

    @pl.when(r > 0)
    def _():
        rs(r, True).wait_recv()

    sum1(1)

    @pl.when(r < R - 1)
    def _():
        rs(r, False).wait_recv()

    has_left = jnp.where(r > 0, 1.0, 0.0)
    has_right = jnp.where(r < R - 1, 1.0, 0.0)

    @pl.when(r > 0)
    def _():
        add_rows(GI, r, RR)

    @pl.when(r < R - 1)
    def _():
        add_rows(GI, r, RL)

    backward_in(0, lambda s: GI[r, s, :].astype(F32))
    sum2(1)
    backward_out(0)
    start(cp1(0))
    arrived(loss2)
    L3[0] = functools.reduce(lambda a, b: a + b, [L2[j] for j in range(C2)])
    start(loss3)
    sum3(1)
    sum1(0)
    share5(1)
    sum2(0)
    share6(1)
    sum3(0)
    out1 = finish(1)
    out1.start()
    share5(0)
    arrived(loss3)
    loss_ref[...] = functools.reduce(lambda a, b: a + b, [L3[j] for j in range(R)])
    share6(0)
    out0 = finish(0)
    out0.start()

    def sent(b, _):
        @pl.when(jnp.logical_and(r < R - 1, b <= r))
        def _():
            ag(b, True).wait_send()

        @pl.when(jnp.logical_and(r > 0, b >= r))
        def _():
            ag(b, False).wait_send()

        @pl.when(b > r)
        def _():
            rs(b, True).wait_send()

        @pl.when(b < r)
        def _():
            rs(b, False).wait_send()

        return 0

    lax.fori_loop(0, R, sent, 0)
    for t in range(2):
        for cps in (cp1(t), cp2(t), cp3(t), cp4(t), cp5(t), cp6(t)):
            for cp in cps:
                cp.wait_send()
    for cp in loss1 + loss2 + loss3:
        cp.wait_send()
    out1.wait()
    out0.wait()


def solution(mesh):
    R, C = mesh.shape["row"], mesh.shape["col"]
    C2 = C // 2

    def body(xu, xi, sharp, pos, w1u, w2u, w1i, w2i):
        M, F = xu.shape
        H, E = w2u.shape
        tiles = (F // 16) * (H // 128) + (H // 16) * (E // 128)
        T = -(-tiles // (R * C))
        NT = T * R * C
        RT = R * T
        hold = R * M * M * 4 <= 1 << 24
        V = pltpu.VMEM
        DMA = pltpu.SemaphoreType.DMA
        hbm = pl.BlockSpec(memory_space=pl.ANY)
        vmem = pl.BlockSpec(memory_space=pltpu.VMEM)
        fin, loss = pl.pallas_call(
            functools.partial(kernel, R, C, T, M, F, H, E, hold),
            name="step",
            out_shape=(
                jax.ShapeDtypeStruct((2, NT, 16, 128), BF16),
                jax.ShapeDtypeStruct((8, 128), F32),
            ),
            in_specs=[hbm, hbm, vmem, vmem, hbm, hbm, hbm, hbm],
            out_specs=(hbm, vmem),
            scratch_shapes=[
                V((2, M, F), BF16), V((2, F, H), BF16), V((2, H, E), BF16),
                V((2, M, H), BF16), V((2, M, E), F32), V((M, E), BF16),
                V((R, M, E), BF16), V((R, M, M) if hold else (1, 8, 128), F32), V((R, M, M), BF16),
                V((R, M, E), BF16), V((R, M, E), BF16), V((R, M, E), BF16),
                V((M, E), F32), V((M, E), BF16), V((M, H), BF16),
                V((1, M), F32), V((1, M), F32),
                V((2, NT, 16, 128), BF16), V((2, NT // 2, 16, 128), BF16),
                V((2, C2 - 1, RT, 16, 128), BF16), V((2, RT, 16, 128), BF16),
                V((2, R - 1, T, 16, 128), BF16), V((2, NT, 16, 128), BF16),
                V((8, 128), F32), V((8, 128), F32), V((C2, 8, 128), F32), V((R, 8, 128), F32),
                DMA((2, 3)), DMA((2,)), DMA((2, R)), DMA((R,)), DMA((R,)), DMA((2, R)),
                DMA((2,)), DMA((2,)), DMA((2, C2 - 1)), DMA((2, C2 - 1)),
                DMA((2, R - 1)), DMA((2, R - 1)), DMA((2, R - 1)), DMA((2, R - 1)),
                DMA((2, C2 - 1)), DMA((2, C2 - 1)), DMA((2,)), DMA((2,)),
                DMA((C2 + R,)), DMA((C2 + R,)),
            ],
            compiler_params=pltpu.CompilerParams(
                collective_id=0, has_side_effects=True, vmem_limit_bytes=67043328
            ),
        )(xu, xi, sharp[None, :], pos[None, :], w1u, w2u, w1i, w2i)

        def unpack(t):
            flat = fin[t].reshape(NT * 16, 128)
            n1 = F * (H // 128)
            n2 = H * (E // 128)
            first = flat[:n1].reshape(H // 128, F, 128).transpose(1, 0, 2).reshape(F, H)
            second = flat[n1 : n1 + n2].reshape(E // 128, H, 128).transpose(1, 0, 2).reshape(H, E)
            return first.astype(F32), second.astype(F32)

        i1, i2 = unpack(0)
        u1, u2 = unpack(1)
        return (loss[0, 0] / (M * R * C), u1, u2, i1, i2)

    placed = (
        P(("row", "col"), None), P(("row", "col"), None), P(("row", "col")), P(("row", "col")),
        P(), P(), P(), P(),
    )
    return jax.shard_map(
        body, mesh=mesh, in_specs=placed, out_specs=(P(), P(), P(), P(), P()), check_vma=False
    )
```

time: 293 us -> 158 us (0.54)
  Pallas kernels: 0 us -> 146 us
  waiting for transfers between devices: 128 us -> 0 us
  blocking collectives: 81.1 us -> 0 us
  matrix products: 43.5 us -> 0 us
  between operations: 15.7 us -> 2.43 us
  other arithmetic: 11.6 us -> 3.61 us
  local copies, waits for them, and re-layouts: 12.6 us -> 5.44 us
    pallas_call x0 -> x1, Pallas kernels: none -> 146 us  [body(): pl.pallas_call(functools.partial(kernel, R, C, T, M, F, H, E, hold), name...]
    psum x1 -> x0, waiting for transfers between devices: 108 us -> none  [body(): lax.psum((grad_user_first, grad_user_second, grad_item_first, grad_item_s...]
    dot_general x11 -> x0, matrix products: 43.5 us -> none  [the longest x1 10.3 us: body(): jnp.einsum('ui,ue->ie', group_dlogits, all_users, preferred_element_type=...]
    all_gather x3 -> x0, blocking collectives: 41.5 us -> none  [the longest x1 14.1 us: body(): lax.all_gather(affinity_sharpness, 'row', axis=0, tiled=True)]
    psum x1 -> x0, blocking collectives: 39.7 us -> none  [body(): lax.psum((grad_user_first, grad_user_second, grad_item_first, grad_item_s...]
    all_gather x2 -> x0, waiting for transfers between devices: 20.4 us -> none  [the longest x1 14.8 us: body(): lax.all_gather(offered_thing_vector, 'row', axis=0, tiled=True)]
    unnamed x36 -> x0, local copies, waits for them, and re-layouts: 12.6 us -> none
    reduce_sum x2 -> x0, other arithmetic: 7.49 us -> none  [the longest x1 6.88 us: positive_pair_logit(): picked = jnp.sum(jnp.where(target_column, affinity_matrix, 0.0), axis=1)]
  transfers between devices with their start and end apart: 3 -> 0, of which waited for: 3 -> 0; matrix products, arithmetic and copies ran while one was open for 10% -> 0% of each run, Pallas kernels for 0% -> 0%
where the time goes in v1:
time: 158 us; the launch traced here: 157 us
  Pallas kernels  146 us (92%)
  local copies, waits for them, and re-layouts  5.44 us (3%)
  other arithmetic  3.61 us (2%)
  between operations  2.43 us (2%)
    pallas_call x1, Pallas kernels, body(): pl.pallas_call(functools.partial(kernel, R, C, T, M, F, H, E, hold), name...  146 us
    convert_element_type x2, other arithmetic, unpack(): return (first.astype(F32), second.astype(F32))  3.61 us

profile of v1, /device:TPU:0, one launch (start us, length us, event | category | flops | bytes accessed | tf_op | source)
XLA Modules:
  0.0 157.4 jit_solution(12339595117584601627)
XLA Ops:
  0.6 1.3 broadcast_in_dim.6.sharp_ref
  1.9 145.9 %step.1 = (bf16[2,320,16,128]{3,2,1,0:T(8,128)(2,1)}, f32[8,128]{1,0:T(8,128)}) custom-call(bf16[1024,1024]{1,0:T(8,128)(2,1)} %xu_hbm.1, bf16[1024,1024]{1,0:T(8,128)(2,1)} %xi_hbm.1, bf16[1,1024]{1,0:T(2,128)(2,1)} %broadcast_in_dim.6.sharp_ref, s32[1,1024]{1,0:T(1,128)} %bitcast.38, bf16[1024,512]{1,0:T(8,128)(2,1)} %w1u_hbm.1, bf16[512,256]{1,0:T(8,128)(2,1)} %w2u_hbm.1, ...), custom_call_target="tpu_custom_call" | custom-call | tf_op jit(solution)/shard_map/step/pallas_call | solution.py:499
  147.8 1.2 slice.25
  149.6 1.1 fusion
  150.7 1.9 %fusion.1 = (bf16[1,256,16,128]{3,2,1,0:T(8,128)(2,1)S(1)}, bf16[1,256,16,128]{3,2,1,0:T(8,128)(2,1)S(1)}) fusion(bf16[2,320,16,128]{3,2,1,0:T(8,128)(2,1)} %get-tuple-element.8), kind=kLoop, calls=%fused_computation.9 | loop fusion | bytes 4194304 | tf_op jit(solution)/shard_map/slice | solution.py:534
  152.6 1.0 copy_bitcast_fusion.2
  153.7 2.6 %copy_bitcast_fusion = (f32[1024,512]{1,0:T(8,128)}, f32[1024,512]{1,0:T(8,128)}) fusion(bf16[4,1024,128]{2,1,0:T(8,128)(2,1)S(1)} %bitcast.35, bf16[4,1024,128]{2,1,0:T(8,128)(2,1)S(1)} %bitcast.34), kind=kLoop, calls=%fused_computation | loop fusion | flops 1048576 | bytes 6291456 | tf_op jit(solution)/shard_map/convert_element_type | solution.py:536

commit v2 on v1

--- a/solution.py
+++ b/solution.py
@@ -23,11 +23,12 @@
     xu_hbm, xi_hbm, sharp_ref, pos_ref, w1u_hbm, w2u_hbm, w1i_hbm, w2i_hbm,
     fin_hbm, loss_ref,
     X, W1, W2, HID, OUT, U, IT, EX, D, GI, RR, RL, GU, GV, GP, LS, PK,
-    B, P1, P2, S2, P3, FIN, L0, L1, L2, L3,
+    B, P1, P2, S2, P3, FIN, L0, L1, L2, L3, FS, PS, SUMS, OTHER,
     in_sem, out_sem, ag_send, ag_recv, rs_send, rs_recv,
-    c1s, c1r, c2s, c2r, c3s, c3r, c4s, c4r, c5s, c5r, c6s, c6r, ls, lr,
+    c1s, c1r, c2s, c2r, c3s, c3r, c4s, c4r, c5s, c5r, c6s, c6r, ls, lr, sq_send, sq_recv,
 ):
     C2 = C // 2
+    square = R == 4 and hold
     r = lax.axis_index("row")
     c = lax.axis_index("col")
     core = lax.rem(c, 2)
@@ -73,176 +74,352 @@
         cp.wait()
 
     def put_item(s, v):
-        IT[r, s, :] = v
+        IT[0 if square else r, s, :] = v
 
     forward(0, put_item)
     pl.semaphore_wait(barrier, R + C2 - 1)
 
-    def ag(b, right):
-        d = 1 if right else 0
-        return pltpu.make_async_remote_copy(
-            src_ref=IT.at[b], dst_ref=IT.at[b], send_sem=ag_send.at[d, b], recv_sem=ag_recv.at[b],
-            device_id=(r + 1 if right else r - 1, c), device_id_type=MESH,
-        )
-
-    @pl.when(r < R - 1)
-    def _():
-        ag(r, True).start()
-
-    @pl.when(r > 0)
-    def _():
-        ag(r, False).start()
-
-    for cp in loads[3:]:
-        cp.wait()
-
-    def put_user(s, v):
-        U[s, :] = v
-
-    forward(1, put_user)
-    LS[...] = jnp.zeros_like(LS)
-    PK[...] = jnp.zeros_like(PK)
-    factor = sharp_ref[...].astype(F32) * (1.0 / E)
-    positive = pos_ref[...]
-
-    def score(b):
-        def step(i, _):
-            s = rows(i)
-            logit = mm(IT[b, s, :], U[...], 1, 1) * factor
-            item = lax.broadcasted_iota(jnp.int32, logit.shape, 0) + (b * M + i * TILE)
-            e = jnp.exp(logit)
-            if hold:
-                EX[b, s, :] = e
-            LS[...] += jnp.sum(e, axis=0, keepdims=True)
-            PK[...] += jnp.sum(jnp.where(item == positive, logit, 0.0), axis=0, keepdims=True)
-            return 0
-
-        lax.fori_loop(0, M // TILE, step, 0)
-
-    score(r)
-
-    def arrive(d, _):
-        lo = r - d
-        hi = r + d
-
-        @pl.when(lo >= 0)
-        def _():
-            ag(lo, True).wait_recv()
-
-            @pl.when(r < R - 1)
-            def _():
-                ag(lo, True).start()
-
-        @pl.when(hi < R)
-        def _():
-            ag(hi, False).wait_recv()
-
-            @pl.when(r > 0)
-            def _():
-                ag(hi, False).start()
-
-        def one(k, _):
-            b = lo + k * (hi - lo)
-
-            @pl.when(jnp.logical_and(b >= 0, b < R))
-            def _():
-                score(b)
-
-            return 0
-
-        lax.fori_loop(0, 2, one, 0)
-        return 0
-
-    lax.fori_loop(1, R, arrive, 0)
-
-    L0[...] = jnp.full(L0.shape, jnp.sum(jnp.log(LS[...]) - PK[...]), F32)
-    GU[...] = jnp.zeros_like(GU)
-    rate = factor * (1.0 / M)
-    norm = 1.0 / LS[...]
-
-    def back(b):
-        def step(i, _):
-            s = rows(i)
-            item = lax.broadcasted_iota(jnp.int32, (TILE, M), 0) + (b * M + i * TILE)
-            hit = jnp.where(item == positive, 1.0, 0.0)
-            e = EX[b, s, :] if hold else jnp.exp(mm(IT[b, s, :], U[...], 1, 1) * factor)
-            d = ((e * norm - hit) * rate).astype(BF16)
-            D[b, s, :] = d
-            GI[b, s, :] = mm(d, U[...]).astype(BF16)
-            return 0
-
-        lax.fori_loop(0, M // TILE, step, 0)
-
-    def rs(b, right):
-        d = 1 if right else 0
-        land = RR if right else RL
-        return pltpu.make_async_remote_copy(
-            src_ref=GI.at[b], dst_ref=land.at[b], send_sem=rs_send.at[b], recv_sem=rs_recv.at[d, b],
-            device_id=(r + 1 if right else r - 1, c), device_id_type=MESH,
-        )
-
-    def leave(k, _):
-        d = R - 1 - k
-        lo = r - d
-        hi = r + d
-
-        def one(q, _):
-            b = hi + q * (lo - hi)
-
-            @pl.when(jnp.logical_and(b >= 0, b < R))
-            def _():
-                back(b)
-
-            return 0
-
-        lax.fori_loop(0, 2, one, 0)
-
-        @pl.when(jnp.logical_and(hi < R, r == 0))
-        def _():
-            rs(hi, True).start()
-
-        @pl.when(jnp.logical_and(lo >= 0, r == R - 1))
-        def _():
-            rs(lo, False).start()
-
-        return 0
-
-    lax.fori_loop(0, R - 1, leave, 0)
-
-    def add_rows(dst, b, land):
-        def step(i, _):
-            s = rows(i)
-            dst[b, s, :] = (dst[b, s, :].astype(F32) + land[b, s, :].astype(F32)).astype(BF16)
-            return 0
-
-        lax.fori_loop(0, M // TILE, step, 0)
-
-    def relay(k):
-        hi = R - 1 - k
-        lo = k
-
-        @pl.when(jnp.logical_and(hi > r, r > 0))
-        def _():
-            rs(hi, True).wait_recv()
-            add_rows(GI, hi, RR)
-            rs(hi, True).start()
-
-        @pl.when(jnp.logical_and(lo < r, r < R - 1))
-        def _():
-            rs(lo, False).wait_recv()
-            add_rows(GI, lo, RL)
-            rs(lo, False).start()
-
-    back(r)
-
-    def user_grad(b, _):
-        def step(i, _):
-            s = rows(i)
-            GU[s, :] += mm(D[b, :, s], IT[b], 0, 0)
-            return 0
-
-        lax.fori_loop(0, M // TILE, step, 0)
-        return 0
+    if square:
+        inner = jnp.logical_or(r == 1, r == 2)
+        outer = jnp.logical_not(inner)
+        side = r // 2
+        buddy = side * 2 + (1 - lax.rem(r, 2))
+        across = 2 - side
+        beyond = 3 - 3 * side
+        first_slot = jnp.where(inner, 1, 0)
+
+        def block_of(slot):
+            near = jnp.where(inner, across, buddy)
+            return jnp.where(slot == 0, r, jnp.where(slot == 1, near, beyond))
+
+        def to(src, dst, k, row, ks=None):
+            return pltpu.make_async_remote_copy(
+                src_ref=src, dst_ref=dst, send_sem=sq_send.at[k if ks is None else ks], recv_sem=sq_recv.at[k],
+                device_id=(row, c), device_id_type=MESH,
+            )
+
+        item_near = to(IT.at[0], IT.at[1], 0, across)
+        item_buddy = to(IT.at[0], IT.at[1], 1, buddy)
+        item_far = to(IT.at[0], IT.at[2], 2, across)
+        user_out = to(U.at[0], U.at[1], 3, buddy)
+        scale_out = to(FS.at[0], FS.at[1], 4, buddy)
+        place_out = to(PS.at[0], PS.at[1], 5, buddy)
+
+        @pl.when(inner)
+        def _():
+            item_near.start()
+            item_buddy.start()
+
+        @pl.when(outer)
+        def _():
+            item_far.start()
+
+        FS[0] = sharp_ref[...].astype(F32) * (1.0 / E)
+        PS[0] = pos_ref[...]
+        for cp in loads[3:]:
+            cp.wait()
+
+        def put_user(s, v):
+            U[0, s, :] = v
+
+        forward(1, put_user)
+        user_out.start()
+        scale_out.start()
+        place_out.start()
+        SUMS[...] = jnp.zeros_like(SUMS)
+
+        def score(q, slot):
+            b = block_of(slot)
+            pair = q * 2 + slot - first_slot
+            factor = FS[q]
+            positive = PS[q]
+
+            def step(i, _):
+                s = rows(i)
+                logit = mm(IT[slot, s, :], U[q], 1, 1) * factor
+                item = lax.broadcasted_iota(jnp.int32, logit.shape, 0) + (b * M + i * TILE)
+                e = jnp.exp(logit)
+                EX[pair, s, :] = e
+                SUMS[q] += jnp.sum(e, axis=0, keepdims=True)
+                SUMS[2 + q] += jnp.sum(
+                    jnp.where(item == positive, logit, 0.0), axis=0, keepdims=True
+                )
+                return 0
+
+            lax.fori_loop(0, M // TILE, step, 0)
+
+        @pl.when(outer)
+        def _():
+            score(0, 0)
+            item_buddy.wait_recv()
+
+        @pl.when(inner)
+        def _():
+            item_near.wait_recv()
+
+        score(0, 1)
+        scale_out.wait_recv()
+        place_out.wait_recv()
+        user_out.wait_recv()
+        score(1, 1)
+
+        @pl.when(outer)
+        def _():
+            score(1, 0)
+
+        @pl.when(inner)
+        def _():
+            item_far.wait_recv()
+
+            def both(q, _):
+                score(q, 2)
+                return 0
+
+            lax.fori_loop(0, 2, both, 0)
+
+        swap = to(SUMS, OTHER, 6, buddy)
+        swap.start()
+        swap.wait_recv()
+        total0 = SUMS[0] + OTHER[1]
+        total1 = SUMS[1] + OTHER[0]
+        L0[...] = jnp.full(L0.shape, jnp.sum(jnp.log(total0) - (SUMS[2] + OTHER[3])), F32)
+        NORM = (1.0 / total0, 1.0 / total1)
+
+        def back(q, k):
+            b = block_of(first_slot + k)
+            rate = FS[q] * (1.0 / M)
+            positive = PS[q]
+
+            def step(i, _):
+                s = rows(i)
+                item = lax.broadcasted_iota(jnp.int32, (TILE, M), 0) + (b * M + i * TILE)
+                hit = jnp.where(item == positive, 1.0, 0.0)
+                D[2 * q + k, s, :] = ((EX[2 * q + k, s, :] * NORM[q] - hit) * rate).astype(BF16)
+                return 0
+
+            lax.fori_loop(0, M // TILE, step, 0)
+
+        def user_part(q, put):
+            def step(i, _):
+                s = rows(i)
+                put(s, mm(D[2 * q, :, s], IT[first_slot], 0, 0)
+                    + mm(D[2 * q + 1, :, s], IT[first_slot + 1], 0, 0))
+                return 0
+
+            lax.fori_loop(0, M // TILE, step, 0)
+
+        def put_sent(s, v):
+            RL[0, s, :] = v.astype(BF16)
+
+        def put_kept(s, v):
+            GU[0, s, :] = v
+
+        user_home = to(RL.at[0], RL.at[1], 7, buddy)
+        back(1, 0)
+        back(1, 1)
+        user_part(1, put_sent)
+        user_home.start()
+        back(0, 0)
+        back(0, 1)
+
+        def item_part(k):
+            def step(i, _):
+                s = rows(i)
+                GI[k, s, :] = (mm(D[k, s, :], U[0]) + mm(D[2 + k, s, :], U[1])).astype(BF16)
+                return 0
+
+            lax.fori_loop(0, M // TILE, step, 0)
+
+        far_home = to(GI.at[1], RR.at[0], 8, beyond, 10)
+        near_home = to(GI.at[0], RR.at[0], 8, across)
+        buddy_home = to(GI.at[1], RR.at[1], 9, buddy)
+        item_part(1)
+
+        @pl.when(inner)
+        def _():
+            far_home.start()
+
+        @pl.when(outer)
+        def _():
+            buddy_home.start()
+
+        item_part(0)
+
+        @pl.when(inner)
+        def _():
+            near_home.start()
+
+        @pl.when(outer)
+        def _():
+            RR[1] = GI[0]
+
+    else:
+
+        def ag(b, right):
+            d = 1 if right else 0
+            return pltpu.make_async_remote_copy(
+                src_ref=IT.at[b], dst_ref=IT.at[b], send_sem=ag_send.at[d, b], recv_sem=ag_recv.at[b],
+                device_id=(r + 1 if right else r - 1, c), device_id_type=MESH,
+            )
+
+        @pl.when(r < R - 1)
+        def _():
+            ag(r, True).start()
+
+        @pl.when(r > 0)
+        def _():
+            ag(r, False).start()
+
+        for cp in loads[3:]:
+            cp.wait()
+
+        def put_user(s, v):
+            U[0, s, :] = v
+
+        forward(1, put_user)
+        LS[...] = jnp.zeros_like(LS)
+        PK[...] = jnp.zeros_like(PK)
+        factor = sharp_ref[...].astype(F32) * (1.0 / E)
+        positive = pos_ref[...]
+
+        def score(b):
+            def step(i, _):
+                s = rows(i)
+                logit = mm(IT[b, s, :], U[0], 1, 1) * factor
+                item = lax.broadcasted_iota(jnp.int32, logit.shape, 0) + (b * M + i * TILE)
+                e = jnp.exp(logit)
+                if hold:
+                    EX[b, s, :] = e
+                LS[...] += jnp.sum(e, axis=0, keepdims=True)
+                PK[...] += jnp.sum(jnp.where(item == positive, logit, 0.0), axis=0, keepdims=True)
+                return 0
+
+            lax.fori_loop(0, M // TILE, step, 0)
+
+        score(r)
+
+        def arrive(d, _):
+            lo = r - d
+            hi = r + d
+
+            @pl.when(lo >= 0)
+            def _():
+                ag(lo, True).wait_recv()
+
+                @pl.when(r < R - 1)
+                def _():
+                    ag(lo, True).start()
+
+            @pl.when(hi < R)
+            def _():
+                ag(hi, False).wait_recv()
+
+                @pl.when(r > 0)
+                def _():
+                    ag(hi, False).start()
+
+            def one(k, _):
+                b = lo + k * (hi - lo)
+
+                @pl.when(jnp.logical_and(b >= 0, b < R))
+                def _():
+                    score(b)
+
+                return 0
+
+            lax.fori_loop(0, 2, one, 0)
+            return 0
+
+        lax.fori_loop(1, R, arrive, 0)
+
+        L0[...] = jnp.full(L0.shape, jnp.sum(jnp.log(LS[...]) - PK[...]), F32)
+        GU[0] = jnp.zeros((M, E), F32)
+        rate = factor * (1.0 / M)
+        norm = 1.0 / LS[...]
+
+        def back(b):
+            def step(i, _):
+                s = rows(i)
+                item = lax.broadcasted_iota(jnp.int32, (TILE, M), 0) + (b * M + i * TILE)
+                hit = jnp.where(item == positive, 1.0, 0.0)
+                e = EX[b, s, :] if hold else jnp.exp(mm(IT[b, s, :], U[0], 1, 1) * factor)
+                d = ((e * norm - hit) * rate).astype(BF16)
+                D[b, s, :] = d
+                GI[b, s, :] = mm(d, U[0]).astype(BF16)
+                return 0
+
+            lax.fori_loop(0, M // TILE, step, 0)
+
+        def rs(b, right):
+            d = 1 if right else 0
+            land = RR if right else RL
+            return pltpu.make_async_remote_copy(
+                src_ref=GI.at[b], dst_ref=land.at[b], send_sem=rs_send.at[b], recv_sem=rs_recv.at[d, b],
+                device_id=(r + 1 if right else r - 1, c), device_id_type=MESH,
+            )
+
+        def leave(k, _):
+            d = R - 1 - k
+            lo = r - d
+            hi = r + d
+
+            def one(q, _):
+                b = hi + q * (lo - hi)
+
+                @pl.when(jnp.logical_and(b >= 0, b < R))
+                def _():
+                    back(b)
+
+                return 0
+
+            lax.fori_loop(0, 2, one, 0)
+
+            @pl.when(jnp.logical_and(hi < R, r == 0))
+            def _():
+                rs(hi, True).start()
+
+            @pl.when(jnp.logical_and(lo >= 0, r == R - 1))
+            def _():
+                rs(lo, False).start()
+
+            return 0
+
+        lax.fori_loop(0, R - 1, leave, 0)
+
+        def add_rows(dst, b, land):
+            def step(i, _):
+                s = rows(i)
+                dst[b, s, :] = (dst[b, s, :].astype(F32) + land[b, s, :].astype(F32)).astype(BF16)
+                return 0
+
+            lax.fori_loop(0, M // TILE, step, 0)
+
+        def relay(k):
+            hi = R - 1 - k
+            lo = k
+
+            @pl.when(jnp.logical_and(hi > r, r > 0))
+            def _():
+                rs(hi, True).wait_recv()
+                add_rows(GI, hi, RR)
+                rs(hi, True).start()
+
+            @pl.when(jnp.logical_and(lo < r, r < R - 1))
+            def _():
+                rs(lo, False).wait_recv()
+                add_rows(GI, lo, RL)
+                rs(lo, False).start()
+
+        back(r)
+
+        def user_grad(b, _):
+            def step(i, _):
+                s = rows(i)
+                GU[0, s, :] += mm(D[b, :, s], IT[b], 0, 0)
+                return 0
+
+            lax.fori_loop(0, M // TILE, step, 0)
+            return 0
 
     def backward_in(t, grad):
         def step(i, _):
@@ -391,44 +568,68 @@
     loss3 = [remote(L3.at[0], L3.at[j], ls.at[C2 - 1 + j], lr.at[C2 - 1 + j], (lax.rem(r + j, R), c))
              for j in range(1, R)]
 
-    start(loss1)
-    relay(0)
-    lax.fori_loop(0, R, user_grad, 0)
-    if R > 2:
-        relay(1)
-    backward_in(1, lambda s: GU[s, :].astype(BF16).astype(F32))
-    if R > 3:
-        relay(2)
-    backward_out(1)
-    start(cp1(1))
-    for k in range(3, R - 1):
-        relay(k)
-    arrived(loss1)
-    L2[0] = L0[...] + L1[...]
-    start(loss2)
-
-    @pl.when(r > 0)
-    def _():
-        rs(r, True).wait_recv()
-
-    sum1(1)
-
-    @pl.when(r < R - 1)
-    def _():
-        rs(r, False).wait_recv()
-
-    has_left = jnp.where(r > 0, 1.0, 0.0)
-    has_right = jnp.where(r < R - 1, 1.0, 0.0)
-
-    @pl.when(r > 0)
-    def _():
-        add_rows(GI, r, RR)
-
-    @pl.when(r < R - 1)
-    def _():
-        add_rows(GI, r, RL)
-
-    backward_in(0, lambda s: GI[r, s, :].astype(F32))
+    if square:
+        start(loss1)
+        user_part(0, put_kept)
+        user_home.wait_recv()
+        backward_in(
+            1, lambda s: (GU[0, s, :] + RL[1, s, :].astype(F32)).astype(BF16).astype(F32)
+        )
+        backward_out(1)
+        start(cp1(1))
+        arrived(loss1)
+        L2[0] = L0[...] + L1[...]
+        start(loss2)
+        sum1(1)
+        near_home.wait_recv()
+
+        @pl.when(inner)
+        def _():
+            buddy_home.wait_recv()
+
+        backward_in(
+            0,
+            lambda s: (RR[0, s, :].astype(F32) + RR[1, s, :].astype(F32)).astype(BF16).astype(F32),
+        )
+    else:
+        start(loss1)
+        relay(0)
+        lax.fori_loop(0, R, user_grad, 0)
+        if R > 2:
+            relay(1)
+        backward_in(1, lambda s: GU[0, s, :].astype(BF16).astype(F32))
+        if R > 3:
+            relay(2)
+        backward_out(1)
+        start(cp1(1))
+        for k in range(3, R - 1):
+            relay(k)
+        arrived(loss1)
+        L2[0] = L0[...] + L1[...]
+        start(loss2)
+
+        @pl.when(r > 0)
+        def _():
+            rs(r, True).wait_recv()
+
+        sum1(1)
+
+        @pl.when(r < R - 1)
+        def _():
+            rs(r, False).wait_recv()
+
+        has_left = jnp.where(r > 0, 1.0, 0.0)
+        has_right = jnp.where(r < R - 1, 1.0, 0.0)
+
+        @pl.when(r > 0)
+        def _():
+            add_rows(GI, r, RR)
+
+        @pl.when(r < R - 1)
+        def _():
+            add_rows(GI, r, RL)
+
+        backward_in(0, lambda s: GI[r, s, :].astype(F32))
     sum2(1)
     backward_out(0)
     start(cp1(0))
@@ -450,26 +651,42 @@
     out0 = finish(0)
     out0.start()
 
-    def sent(b, _):
-        @pl.when(jnp.logical_and(r < R - 1, b <= r))
-        def _():
-            ag(b, True).wait_send()
-
-        @pl.when(jnp.logical_and(r > 0, b >= r))
-        def _():
-            ag(b, False).wait_send()
-
-        @pl.when(b > r)
-        def _():
-            rs(b, True).wait_send()
-
-        @pl.when(b < r)
-        def _():
-            rs(b, False).wait_send()
-
-        return 0
-
-    lax.fori_loop(0, R, sent, 0)
+    if square:
+
+        @pl.when(inner)
+        def _():
+            for cp in (item_near, item_buddy, far_home, near_home):
+                cp.wait_send()
+
+        @pl.when(outer)
+        def _():
+            item_far.wait_send()
+            buddy_home.wait_send()
+
+        for cp in (user_out, scale_out, place_out, swap, user_home):
+            cp.wait_send()
+    else:
+
+        def sent(b, _):
+            @pl.when(jnp.logical_and(r < R - 1, b <= r))
+            def _():
+                ag(b, True).wait_send()
+
+            @pl.when(jnp.logical_and(r > 0, b >= r))
+            def _():
+                ag(b, False).wait_send()
+
+            @pl.when(b > r)
+            def _():
+                rs(b, True).wait_send()
+
+            @pl.when(b < r)
+            def _():
+                rs(b, False).wait_send()
+
+            return 0
+
+        lax.fori_loop(0, R, sent, 0)
     for t in range(2):
         for cps in (cp1(t), cp2(t), cp3(t), cp4(t), cp5(t), cp6(t)):
             for cp in cps:
@@ -478,6 +695,17 @@
         cp.wait_send()
     out1.wait()
     out0.wait()
+
+
+def block_at(t, start, i):
+    return (t, start + i, 0)
+
+
+def unpack(n, *refs):
+    src, dst = list(refs[:n]), refs[n:]
+    for out in dst:
+        for k in range(out.shape[1] // 128):
+            out[:, k * 128 : (k + 1) * 128] = src.pop(0)[0].astype(F32)
 
 
 def solution(mesh):
@@ -507,36 +735,50 @@
             out_specs=(hbm, vmem),
             scratch_shapes=[
                 V((2, M, F), BF16), V((2, F, H), BF16), V((2, H, E), BF16),
-                V((2, M, H), BF16), V((2, M, E), F32), V((M, E), BF16),
+                V((2, M, H), BF16), V((2, M, E), F32), V((2, M, E), BF16),
                 V((R, M, E), BF16), V((R, M, M) if hold else (1, 8, 128), F32), V((R, M, M), BF16),
                 V((R, M, E), BF16), V((R, M, E), BF16), V((R, M, E), BF16),
-                V((M, E), F32), V((M, E), BF16), V((M, H), BF16),
+                V((2, M, E), F32), V((M, E), BF16), V((M, H), BF16),
                 V((1, M), F32), V((1, M), F32),
                 V((2, NT, 16, 128), BF16), V((2, NT // 2, 16, 128), BF16),
                 V((2, C2 - 1, RT, 16, 128), BF16), V((2, RT, 16, 128), BF16),
                 V((2, R - 1, T, 16, 128), BF16), V((2, NT, 16, 128), BF16),
                 V((8, 128), F32), V((8, 128), F32), V((C2, 8, 128), F32), V((R, 8, 128), F32),
+                V((2, 1, M), F32), V((2, 1, M), jnp.int32), V((4, 1, M), F32), V((4, 1, M), F32),
                 DMA((2, 3)), DMA((2,)), DMA((2, R)), DMA((R,)), DMA((R,)), DMA((2, R)),
                 DMA((2,)), DMA((2,)), DMA((2, C2 - 1)), DMA((2, C2 - 1)),
                 DMA((2, R - 1)), DMA((2, R - 1)), DMA((2, R - 1)), DMA((2, R - 1)),
                 DMA((2, C2 - 1)), DMA((2, C2 - 1)), DMA((2,)), DMA((2,)),
-                DMA((C2 + R,)), DMA((C2 + R,)),
+                DMA((C2 + R,)), DMA((C2 + R,)), DMA((11,)), DMA((11,)),
             ],
             compiler_params=pltpu.CompilerParams(
                 collective_id=0, has_side_effects=True, vmem_limit_bytes=67043328
             ),
         )(xu, xi, sharp[None, :], pos[None, :], w1u, w2u, w1i, w2i)
 
-        def unpack(t):
-            flat = fin[t].reshape(NT * 16, 128)
-            n1 = F * (H // 128)
-            n2 = H * (E // 128)
-            first = flat[:n1].reshape(H // 128, F, 128).transpose(1, 0, 2).reshape(F, H)
-            second = flat[n1 : n1 + n2].reshape(E // 128, H, 128).transpose(1, 0, 2).reshape(H, E)
-            return first.astype(F32), second.astype(F32)
-
-        i1, i2 = unpack(0)
-        u1, u2 = unpack(1)
+        flat = fin.reshape(2, NT * 16, 128)
+        steps = 4
+        specs, outs, shapes = [], [], []
+        for t in range(2):
+            base = 0
+            for height, width in ((F, H), (H, E)):
+                tall = height // steps
+                for k in range(width // 128):
+                    start = (base + k * height) // tall
+                    specs.append(
+                        pl.BlockSpec((1, tall, 128), functools.partial(block_at, t, start))
+                    )
+                base += height * (width // 128)
+                outs.append(pl.BlockSpec((tall, width), lambda i: (i, 0)))
+                shapes.append(jax.ShapeDtypeStruct((height, width), F32))
+        i1, i2, u1, u2 = pl.pallas_call(
+            functools.partial(unpack, len(specs)),
+            name="unpack",
+            grid=(steps,),
+            in_specs=specs,
+            out_specs=outs,
+            out_shape=shapes,
+        )(*([flat] * len(specs)))
         return (loss[0, 0] / (M * R * C), u1, u2, i1, i2)
 
     placed = (

time: 158 us -> 131 us (0.83)
  Pallas kernels: 146 us -> 124 us
  other arithmetic: 3.61 us -> 0 us
  local copies, waits for them, and re-layouts: 5.44 us -> 2.47 us
    pallas_call x1, Pallas kernels: 146 us -> 120 us  [body(): pl.pallas_call(functools.partial(kernel, R, C, T, M, F, H, E, hold), name...]
    pallas_call x0 -> x1, Pallas kernels: none -> 4.72 us  [body(): pl.pallas_call(functools.partial(unpack, len(specs)), name='unpack', grid...]
    convert_element_type x2 -> x0, other arithmetic: 3.61 us -> none  [unpack(): return (first.astype(F32), second.astype(F32))]
    slice x2 -> x0, local copies, waits for them, and re-layouts: 2.97 us -> none  [the longest x1 1.9 us: unpack(): first = flat[:n1].reshape(H // 128, F, 128).transpose(1, 0, 2).reshape(F, H)]
where the time goes in v2:
time: 131 us; the launch traced here: 129 us
  Pallas kernels  124 us (95%)
  local copies, waits for them, and re-layouts  2.47 us (2%)
  between operations  2.42 us (2%)
    pallas_call x1, Pallas kernels, body(): pl.pallas_call(functools.partial(kernel, R, C, T, M, F, H, E, hold), name...  120 us
    pallas_call x1, Pallas kernels, body(): pl.pallas_call(functools.partial(unpack, len(specs)), name='unpack', grid...  4.72 us

profile of v2, /device:TPU:0, one launch (start us, length us, event | category | flops | bytes accessed | tf_op | source)
XLA Modules:
  0.0 129.4 jit_solution(10612180510128617012)
XLA Ops:
  0.6 1.3 broadcast_in_dim.6.sharp_ref
  1.9 119.8 %step.1 = (bf16[2,320,16,128]{3,2,1,0:T(8,128)(2,1)}, f32[8,128]{1,0:T(8,128)}) custom-call(bf16[1024,1024]{1,0:T(8,128)(2,1)} %xu_hbm.1, bf16[1024,1024]{1,0:T(8,128)(2,1)} %xi_hbm.1, bf16[1,1024]{1,0:T(2,128)(2,1)} %broadcast_in_dim.6.sharp_ref, s32[1,1024]{1,0:T(1,128)} %bitcast.15, bf16[1024,512]{1,0:T(8,128)(2,1)} %w1u_hbm.1, bf16[512,256]{1,0:T(8,128)(2,1)} %w2u_hbm.1, ...), custom_call_target="tpu_custom_call" | custom-call | tf_op jit(solution)/shard_map/step/pallas_call | solution.py:727
  121.7 1.2 slice.3
  123.5 4.7 %unpack.1 = (f32[1024,512]{1,0:T(8,128)}, f32[512,256]{1,0:T(8,128)}, f32[1024,512]{1,0:T(8,128)}, f32[512,256]{1,0:T(8,128)}) custom-call(bf16[2,5120,128]{2,1,0:T(8,128)(2,1)} %bitcast.3, bf16[2,5120,128]{2,1,0:T(8,128)(2,1)} %bitcast.4, bf16[2,5120,128]{2,1,0:T(8,128)(2,1)} %bitcast.5, bf16[2,5120,128]{2,1,0:T(8,128)(2,1)} %bitcast.6, ...), custom_call_target="tpu_custom_call" | custom-call | tf_op jit(solution)/shard_map/unpack/pallas_call | solution.py:774

commit v3 on v2

--- a/solution.py
+++ b/solution.py
@@ -581,6 +581,7 @@
         L2[0] = L0[...] + L1[...]
         start(loss2)
         sum1(1)
+        sum2(1)
         near_home.wait_recv()
 
         @pl.when(inner)
@@ -629,18 +630,18 @@
         def _():
             add_rows(GI, r, RL)
 
+        sum2(1)
         backward_in(0, lambda s: GI[r, s, :].astype(F32))
-    sum2(1)
+    sum3(1)
     backward_out(0)
     start(cp1(0))
     arrived(loss2)
     L3[0] = functools.reduce(lambda a, b: a + b, [L2[j] for j in range(C2)])
     start(loss3)
-    sum3(1)
+    share5(1)
     sum1(0)
-    share5(1)
+    share6(1)
     sum2(0)
-    share6(1)
     sum3(0)
     out1 = finish(1)
     out1.start()

time: 131 us -> 139 us (1.061)
  Pallas kernels: 124 us -> 132 us
    pallas_call x1, Pallas kernels: 120 us -> 128 us  [body(): pl.pallas_call(functools.partial(kernel, R, C, T, M, F, H, E, hold), name...]
where the time goes in v3:
time: 139 us; the launch traced here: 137 us
  Pallas kernels  132 us (95%)
  local copies, waits for them, and re-layouts  2.47 us (2%)
  between operations  2.42 us (2%)
    pallas_call x1, Pallas kernels, body(): pl.pallas_call(functools.partial(kernel, R, C, T, M, F, H, E, hold), name...  128 us
    pallas_call x1, Pallas kernels, body(): pl.pallas_call(functools.partial(unpack, len(specs)), name='unpack', grid...  4.72 us

profile of v3, /device:TPU:0, one launch (start us, length us, event | category | flops | bytes accessed | tf_op | source)
XLA Modules:
  0.0 137.3 jit_solution(854466173400719666)
XLA Ops:
  0.6 1.3 broadcast_in_dim.6.sharp_ref
  1.9 127.7 %step.1 = (bf16[2,320,16,128]{3,2,1,0:T(8,128)(2,1)}, f32[8,128]{1,0:T(8,128)}) custom-call(bf16[1024,1024]{1,0:T(8,128)(2,1)} %xu_hbm.1, bf16[1024,1024]{1,0:T(8,128)(2,1)} %xi_hbm.1, bf16[1,1024]{1,0:T(2,128)(2,1)} %broadcast_in_dim.6.sharp_ref, s32[1,1024]{1,0:T(1,128)} %bitcast.15, bf16[1024,512]{1,0:T(8,128)(2,1)} %w1u_hbm.1, bf16[512,256]{1,0:T(8,128)(2,1)} %w2u_hbm.1, ...), custom_call_target="tpu_custom_call" | custom-call | tf_op jit(solution)/shard_map/step/pallas_call | solution.py:728
  129.6 1.2 slice.3
  131.4 4.7 %unpack.1 = (f32[1024,512]{1,0:T(8,128)}, f32[512,256]{1,0:T(8,128)}, f32[1024,512]{1,0:T(8,128)}, f32[512,256]{1,0:T(8,128)}) custom-call(bf16[2,5120,128]{2,1,0:T(8,128)(2,1)} %bitcast.3, bf16[2,5120,128]{2,1,0:T(8,128)(2,1)} %bitcast.4, bf16[2,5120,128]{2,1,0:T(8,128)(2,1)} %bitcast.5, bf16[2,5120,128]{2,1,0:T(8,128)(2,1)} %bitcast.6, ...), custom_call_target="tpu_custom_call" | custom-call | tf_op jit(solution)/shard_map/unpack/pallas_call | solution.py:775
